TPU v7x, 128 devices: a whole 4x4x4 slice. The times are simulated.
128 devices in a mesh: dp: 4 (over x), fy: 4 (over z_hi, core), fx: 8 (over z_lo, y).
Axes of the slice: x: 4, y: 4, z: 4 (z_hi: 2, z_lo: 2; z = z_hi * 2 + z_lo), core: 2. Of those that a mesh axis runs over, the one named last changes fastest.
Arguments:
- fine_tokens: bfloat16 [4, 64, 256, 768], P('dp', 'fy', 'fx'), may hold values from -40 to 40
- parent: int32 [4, 64, 64], P('dp', 'fy', 'fx'), may hold values from 0 to 511, as said below
- coarse_tokens: bfloat16 [4, 512, 768], P('dp', 'fx'), may hold values from -6 to 6
- tile_level: int32 [4, 512], P('dp', 'fx'), may hold values from 0 to 2
- level_table: float32 [3, 768], replicated, may hold values from -3 to 3
- norm_gain: float32 [768], replicated, may hold values from 0.5 to 1.5
- qkv_weight: bfloat16 [768, 2304], replicated, may hold values from -7 to 7
- out_weight: bfloat16 [768, 768], replicated, may hold values from -0.21875 to 0.21875
- cotangent: bfloat16 [4, 64, 256, 768], P('dp', 'fy', 'fx'), may hold values from -6 to 6
Outputs:
- mixed: bfloat16 [4, 64, 256, 768], P('dp', 'fy', 'fx')
- grad_tokens: bfloat16 [4, 64, 256, 768], P('dp', 'fy', 'fx')
- grad_coarse: float32 [4, 512, 768], P('dp', 'fx')
- grad_qkv: float32 [768, 2304], P('dp')
- grad_out: float32 [768, 768], P('dp')
- grad_gain: float32 [768], P('dp')
- grad_level: float32 [3, 768], replicated
Inputs may be any that keep to these rules, and one draw needn't show every extreme that they name: `parent`: each entry names a coarse token of the same frame; a token of level l is drawn with weight l + 1.
All inputs are finite; a program needn't handle non-finite values.
Results may differ from a plain program's by a relative error of at most 0.025.
Values may be sent and summed in bfloat16 or wider, within the bound.
A program may use at most 128 MiB of HBM per device.

v0:
```python
import functools
import math
import jax
import jax.numpy as jnp
from jax import lax
from jax.sharding import PartitionSpec as P

HEADS = 12
BLK = 4
LEVELS = 3


def as_sent(shard):
    return jax.tree.map(lambda a: a.astype(jnp.bfloat16) if a.dtype == jnp.float32 else a, shard)


def attend_forward(queries, key_rows, values, score_scale, query_form, key_form, score_form):
    scores = (
        jnp.einsum(
            query_form + "," + key_form + "->" + score_form,
            queries,
            key_rows,
            preferred_element_type=jnp.float32,
        )
        * score_scale
    )
    weights = jax.nn.softmax(scores, axis=-1)
    rounded = weights.astype(jnp.bfloat16)
    attended = jnp.einsum(
        score_form + "," + key_form + "->" + query_form,
        rounded,
        values,
        preferred_element_type=jnp.float32,
    )
    return attended.astype(jnp.bfloat16)


def attend_grads(
    weights,
    rounded,
    queries,
    key_rows,
    values,
    grad_out,
    score_scale,
    query_form,
    key_form,
    score_form,
):
    grad_values = jnp.einsum(
        score_form + "," + query_form + "->" + key_form,
        rounded,
        grad_out,
        preferred_element_type=jnp.float32,
    ).astype(jnp.bfloat16)
    grad_weights = jnp.einsum(
        query_form + "," + key_form + "->" + score_form,
        grad_out,
        values,
        preferred_element_type=jnp.float32,
    )
    inner = jnp.sum(weights * grad_weights, axis=-1, keepdims=True)
    grad_scores = (weights * (grad_weights - inner) * score_scale).astype(jnp.bfloat16)
    grad_queries = jnp.einsum(
        score_form + "," + key_form + "->" + query_form,
        grad_scores,
        key_rows,
        preferred_element_type=jnp.float32,
    ).astype(jnp.bfloat16)
    grad_keys = jnp.einsum(
        score_form + "," + query_form + "->" + key_form,
        grad_scores,
        queries,
        preferred_element_type=jnp.float32,
    ).astype(jnp.bfloat16)
    return (grad_queries, grad_keys, grad_values)


def attend_backward(
    queries, key_rows, values, grad_out, score_scale, query_form, key_form, score_form
):
    scores = (
        jnp.einsum(
            query_form + "," + key_form + "->" + score_form,
            queries,
            key_rows,
            preferred_element_type=jnp.float32,
        )
        * score_scale
    )
    weights = jax.nn.softmax(scores, axis=-1)
    rounded = weights.astype(jnp.bfloat16)
    return attend_grads(
        weights,
        rounded,
        queries,
        key_rows,
        values,
        grad_out,
        score_scale,
        query_form,
        key_form,
        score_form,
    )


def take_rows(table_rows, row_ids):
    return jnp.take(table_rows, row_ids, axis=0)


def rows_to_batch(tensor, head_dim):
    return tensor.reshape(tensor.shape[1], tensor.shape[2], -1, head_dim)


def batch_to_rows(tensor):
    return tensor.reshape(1, tensor.shape[0], tensor.shape[1], -1)


def columns_to_batch(tensor, head_dim):
    return tensor.reshape(tensor.shape[0], tensor.shape[1], tensor.shape[3], -1, head_dim)


def batch_to_columns(tensor):
    return tensor.reshape(tensor.shape[0], tensor.shape[1], 1, tensor.shape[2], -1)


def to_row_groups(tensor, groups):
    return tensor.reshape(groups, -1, tensor.shape[2], tensor.shape[3])


def to_column_groups(tensor, groups):
    return tensor.reshape(tensor.shape[0], tensor.shape[1], groups, -1, tensor.shape[3])


def local(
    fine_tokens,
    parent,
    coarse_tokens,
    tile_level,
    level_table,
    norm_gain,
    qkv_weight,
    out_weight,
    cotangent,
):
    frame_count, row_count, column_count, model_dim = fine_tokens.shape
    row_groups = lax.axis_size("fx")
    column_groups = lax.axis_size("fy")
    owners_dev = coarse_tokens.shape[1]
    half_width = model_dim // 2
    head_dim = model_dim // HEADS
    score_scale = head_dim ** (-0.5)
    block_count = column_count // BLK
    token_shape = (frame_count, row_count, column_count, half_width)
    level_onehot = (tile_level[:, :, None] == jnp.arange(LEVELS, dtype=jnp.int32)).astype(
        jnp.float32
    )
    level_add = jnp.sum(level_onehot[:, :, :, None] * level_table[None, None, :, :], axis=2)
    summary = (coarse_tokens.astype(jnp.float32) + level_add).astype(jnp.bfloat16)
    shard_piece = lax.all_gather(summary, "fx", axis=1, tiled=True)
    piece_rows = shard_piece.shape[1]
    inside = (parent >= 0) & (parent < piece_rows)
    local_index = jnp.clip(parent, 0, piece_rows - 1)
    picked = jax.vmap(take_rows)(shard_piece, local_index)
    read_rows = jnp.where(inside[..., None], picked.astype(jnp.float32), 0.0)
    spread = jnp.broadcast_to(
        read_rows[:, :, :, None, :], (frame_count, row_count, block_count, BLK, model_dim)
    )
    residual = fine_tokens.astype(jnp.float32) + spread.reshape(
        frame_count, row_count, column_count, model_dim
    )
    inv_rms = lax.rsqrt(jnp.mean(residual * residual, axis=-1, keepdims=True) + 1e-06)
    normed_pre = residual * inv_rms
    normed = (normed_pre * norm_gain).astype(jnp.bfloat16)
    flat_normed = normed.reshape(-1, model_dim)
    projected = jnp.dot(flat_normed, qkv_weight, preferred_element_type=jnp.float32).astype(
        jnp.bfloat16
    )
    projected = projected.reshape(frame_count, row_count, column_count, 3 * model_dim)
    row_query = projected[..., 0:half_width]
    column_query = projected[..., half_width:model_dim]
    row_key = projected[..., model_dim : model_dim + half_width]
    column_key = projected[..., model_dim + half_width : 2 * model_dim]
    row_value = projected[..., 2 * model_dim : 2 * model_dim + half_width]
    column_value = projected[..., 2 * model_dim + half_width : 3 * model_dim]
    flat_cot = cotangent.reshape(-1, model_dim)
    grad_att = jnp.dot(flat_cot, out_weight.T, preferred_element_type=jnp.float32).astype(
        jnp.bfloat16
    )
    grad_att = grad_att.reshape(frame_count, row_count, column_count, model_dim)
    row_grad_out = grad_att[..., 0:half_width]
    column_grad_out = grad_att[..., half_width:model_dim]
    queries = lax.all_to_all(
        to_row_groups(row_query, row_groups), "fx", split_axis=0, concat_axis=2, tiled=True
    )
    key_rows = lax.all_to_all(
        to_row_groups(row_key, row_groups), "fx", split_axis=0, concat_axis=2, tiled=True
    )
    values = lax.all_to_all(
        to_row_groups(row_value, row_groups), "fx", split_axis=0, concat_axis=2, tiled=True
    )
    attended_rows = attend_forward(
        rows_to_batch(queries, head_dim),
        rows_to_batch(key_rows, head_dim),
        rows_to_batch(values, head_dim),
        score_scale,
        "bqhd",
        "bkhd",
        "bhqk",
    )
    row_out = lax.all_to_all(
        batch_to_rows(attended_rows), "fx", split_axis=2, concat_axis=0, tiled=True
    )
    row_out = row_out.reshape(token_shape)
    queries = lax.all_to_all(
        to_column_groups(column_query, column_groups), "fy", split_axis=2, concat_axis=1, tiled=True
    )
    key_rows = lax.all_to_all(
        to_column_groups(column_key, column_groups), "fy", split_axis=2, concat_axis=1, tiled=True
    )
    values = lax.all_to_all(
        to_column_groups(column_value, column_groups), "fy", split_axis=2, concat_axis=1, tiled=True
    )
    attended_columns = attend_forward(
        columns_to_batch(queries, head_dim),
        columns_to_batch(key_rows, head_dim),
        columns_to_batch(values, head_dim),
        score_scale,
        "fqchd",
        "fkchd",
        "fchqk",
    )
    column_out = lax.all_to_all(
        batch_to_columns(attended_columns), "fy", split_axis=1, concat_axis=2, tiled=True
    )
    column_out = column_out.reshape(token_shape)
    queries = lax.all_to_all(
        to_row_groups(row_query, row_groups), "fx", split_axis=0, concat_axis=2, tiled=True
    )
    key_rows = lax.all_to_all(
        to_row_groups(row_key, row_groups), "fx", split_axis=0, concat_axis=2, tiled=True
    )
    values = lax.all_to_all(
        to_row_groups(row_value, row_groups), "fx", split_axis=0, concat_axis=2, tiled=True
    )
    grad_rows = lax.all_to_all(
        to_row_groups(row_grad_out, row_groups), "fx", split_axis=0, concat_axis=2, tiled=True
    )
    grads = attend_backward(
        rows_to_batch(queries, head_dim),
        rows_to_batch(key_rows, head_dim),
        rows_to_batch(values, head_dim),
        rows_to_batch(grad_rows, head_dim),
        score_scale,
        "bqhd",
        "bkhd",
        "bhqk",
    )
    row_back = (
        lax.all_to_all(batch_to_rows(grads[0]), "fx", split_axis=2, concat_axis=0, tiled=True),
        lax.all_to_all(batch_to_rows(grads[1]), "fx", split_axis=2, concat_axis=0, tiled=True),
        lax.all_to_all(batch_to_rows(grads[2]), "fx", split_axis=2, concat_axis=0, tiled=True),
    )
    queries = lax.all_to_all(
        to_column_groups(column_query, column_groups), "fy", split_axis=2, concat_axis=1, tiled=True
    )
    key_rows = lax.all_to_all(
        to_column_groups(column_key, column_groups), "fy", split_axis=2, concat_axis=1, tiled=True
    )
    values = lax.all_to_all(
        to_column_groups(column_value, column_groups), "fy", split_axis=2, concat_axis=1, tiled=True
    )
    grad_columns = lax.all_to_all(
        to_column_groups(column_grad_out, column_groups),
        "fy",
        split_axis=2,
        concat_axis=1,
        tiled=True,
    )
    grads = attend_backward(
        columns_to_batch(queries, head_dim),
        columns_to_batch(key_rows, head_dim),
        columns_to_batch(values, head_dim),
        columns_to_batch(grad_columns, head_dim),
        score_scale,
        "fqchd",
        "fkchd",
        "fchqk",
    )
    column_back = (
        lax.all_to_all(batch_to_columns(grads[0]), "fy", split_axis=1, concat_axis=2, tiled=True),
        lax.all_to_all(batch_to_columns(grads[1]), "fy", split_axis=1, concat_axis=2, tiled=True),
        lax.all_to_all(batch_to_columns(grads[2]), "fy", split_axis=1, concat_axis=2, tiled=True),
    )
    attended = jnp.concatenate([row_out, column_out], axis=-1)
    flat_att = attended.reshape(-1, model_dim)
    out_proj = jnp.dot(flat_att, out_weight, preferred_element_type=jnp.float32)
    mixed = (residual + out_proj.reshape(frame_count, row_count, column_count, model_dim)).astype(
        jnp.bfloat16
    )
    grad_out_local = jnp.dot(flat_att.T, flat_cot, preferred_element_type=jnp.float32)
    pieces = []
    for which in range(3):
        pieces.append(row_back[which].reshape(token_shape))
        pieces.append(column_back[which].reshape(token_shape))
    grad_projected = jnp.concatenate(pieces, axis=-1).reshape(-1, 3 * model_dim)
    grad_normed = jnp.dot(grad_projected, qkv_weight.T, preferred_element_type=jnp.float32)
    grad_qkv_local = jnp.dot(flat_normed.T, grad_projected, preferred_element_type=jnp.float32)
    flat_pre = normed_pre.reshape(-1, model_dim)
    grad_gain_local = jnp.sum(grad_normed * flat_pre, axis=0)
    grad_pre = grad_normed * norm_gain
    flat_inv = inv_rms.reshape(-1, 1)
    grad_residual = flat_inv * (
        grad_pre - flat_pre * jnp.mean(grad_pre * flat_pre, axis=-1, keepdims=True)
    ) + flat_cot.astype(jnp.float32)
    grad_fine = grad_residual.astype(jnp.bfloat16).reshape(
        frame_count, row_count, column_count, model_dim
    )
    block_grad = (
        grad_residual.reshape(frame_count, row_count, block_count, BLK, model_dim)
        .sum(axis=3)
        .reshape(frame_count, -1, model_dim)
    )
    parent_flat = parent.reshape(frame_count, -1)
    coarse_total = owners_dev * row_groups
    segment_rows = functools.partial(jax.ops.segment_sum, num_segments=coarse_total)
    dense_sum = jax.vmap(segment_rows)(block_grad, parent_flat)
    owned_rows = jax.tree.map(
        lambda part: part.astype(jnp.float32),
        lax.psum_scatter(as_sent(dense_sum), "fx", scatter_dimension=1, tiled=True),
    )
    grad_coarse = jax.tree.map(
        lambda part: part.astype(jnp.float32), lax.psum(as_sent(owned_rows), "fy")
    )
    level_part = jnp.sum(level_onehot[:, :, :, None] * grad_coarse[:, :, None, :], axis=(0, 1))
    grad_level = lax.psum(level_part, ("dp", "fx"))
    summed = (
        lax.psum(grad_qkv_local.astype(jnp.bfloat16), ("fy", "fx")).astype(jnp.float32),
        lax.psum(grad_out_local.astype(jnp.bfloat16), ("fy", "fx")).astype(jnp.float32),
        lax.psum(grad_gain_local.astype(jnp.bfloat16), ("fy", "fx")).astype(jnp.float32),
    )
    shares = (
        lax.psum_scatter(
            summed[0].astype(jnp.bfloat16), "dp", scatter_dimension=0, tiled=True
        ).astype(jnp.float32),
        lax.psum_scatter(
            summed[1].astype(jnp.bfloat16), "dp", scatter_dimension=0, tiled=True
        ).astype(jnp.float32),
        lax.psum_scatter(
            summed[2].astype(jnp.bfloat16), "dp", scatter_dimension=0, tiled=True
        ).astype(jnp.float32),
    )
    total_tokens = (
        frame_count * row_count * column_count * lax.axis_size("dp") * column_groups * row_groups
    )
    grad_scale = 1.0 / math.sqrt(total_tokens)
    return (
        mixed,
        grad_fine,
        grad_coarse,
        shares[0] * grad_scale,
        shares[1] * grad_scale,
        shares[2] * grad_scale,
        grad_level * grad_scale,
    )


def solution(mesh):
    return jax.shard_map(
        local,
        mesh=mesh,
        in_specs=(
            P("dp", "fy", "fx", None),
            P("dp", "fy", "fx"),
            P("dp", "fx", None),
            P("dp", "fx"),
            P(),
            P(),
            P(),
            P(),
            P("dp", "fy", "fx", None),
        ),
        out_specs=(
            P("dp", "fy", "fx", None),
            P("dp", "fy", "fx", None),
            P("dp", "fx", None),
            P("dp", None),
            P("dp", None),
            P("dp"),
            P(),
        ),
        check_vma=False,
    )
```

profile of v0, /device:TPU:0, one launch (start us, length us, event | category | flops | bytes accessed | tf_op | source)
XLA Modules:
  0.0 606.6 jit_solution(17159746881032802387)
XLA Ops:
  8.0 2.5 convolution_convert_fusion.1
  12.2 5.3 all-to-all-start.10
  23.4 31.8 %all_gather.3 = bf16[1,512,768]{2,1,0:T(8,128)(2,1)} all-gather(bf16[1,64,768]{2,1,0:T(8,128)(2,1)S(1)} %fusion.66), channel_id=1, replica_groups=mesh['dp'=4,'fy'=4,'fx'=8] {'fx'}, dimensions={1}, use_global_device_ids=true | all-gather | bytes 884736 | tf_op jit(solution)/shard_map/all_gather | solution.py:160
  55.2 2.8 gather_fusion
  60.5 2.8 broadcast_in_dim.39
  71.1 5.4 all-to-all-start.6
  78.3 7.2 %all-to-all-done.6 = bf16[1,16,4,8,384]{4,3,1,0,2:T(8,128)(2,1)} async-done(((bf16[1,16,4,8,384]{4,3,1,0,2:T(8,128)(2,1)}), bf16[1,16,4,8,384]{4,3,1,0,2:T(8,128)(2,1)}, u32[]{:S(2)}, u32[]{:S(2)}) %all-to-all-start.6) | async-done | bytes 393248 | tf_op jit(solution)/shard_map/all_to_all | solution.py:218
  85.5 4.1 all-to-all-start.5
  91.4 7.2 %all-to-all-done.5 = bf16[1,16,4,8,384]{4,3,1,0,2:T(8,128)(2,1)} async-done(((bf16[1,16,4,8,384]{4,3,1,0,2:T(8,128)(2,1)}), bf16[1,16,4,8,384]{4,3,1,0,2:T(8,128)(2,1)}, u32[]{:S(2)}, u32[]{:S(2)}) %all-to-all-start.5) | async-done | bytes 393248 | tf_op jit(solution)/shard_map/all_to_all | solution.py:215
  98.6 13.2 %all_to_all.270 = bf16[1,16,4,8,384]{4,3,1,0,2:T(8,128)(2,1)} all-to-all(bf16[1,16,4,8,384]{4,3,1,0,2:T(8,128)(2,1)} %copy.222), channel_id=1, replica_groups=mesh['dp'=4,'fy'=4,'fx'=8] {'fy'}, dimensions={2} | all-to-all | bytes 786432 | tf_op jit(solution)/shard_map/all_to_all | solution.py:221
  111.8 12.7 %all_to_all.271 = bf16[8,2,32,384]{3,2,1,0:T(8,128)(2,1)} all-to-all(bf16[8,2,32,384]{3,2,1,0:T(8,128)(2,1)} %bitcast.260), channel_id=1, replica_groups=mesh['dp'=4,'fy'=4,'fx'=8] {'fx'}, dimensions={0} | all-to-all | bytes 786432 | tf_op jit(solution)/shard_map/all_to_all | solution.py:246
  124.5 11.1 %all_to_all.272 = bf16[8,2,32,384]{3,2,1,0:T(8,128)(2,1)} all-to-all(bf16[8,2,32,384]{3,2,1,0:T(8,128)(2,1)S(1)} %bitcast.251), channel_id=1, replica_groups=mesh['dp'=4,'fy'=4,'fx'=8] {'fx'}, dimensions={0} | all-to-all | bytes 786432 | tf_op jit(solution)/shard_map/all_to_all | solution.py:196
  135.6 4.1 all-to-all-start.1
  139.7 2.4 reshape.396
  142.1 2.7 copy.260
  144.7 2.4 reshape.383
  147.1 2.5 reshape.385
  149.6 2.7 copy.251
  152.3 2.5 reshape.387
  154.7 2.7 copy.242
  157.4 3.3 fusion.59
  160.7 6.1 %all-to-all-start = ((bf16[8,2,32,384]{3,2,1,0:T(8,128)(2,1)}), bf16[8,2,32,384]{3,2,1,0:T(8,128)(2,1)}, u32[]{:S(2)}, u32[]{:S(2)}) async-start(bf16[8,2,32,384]{3,2,1,0:T(8,128)(2,1)} %bitcast.249), calls=%async_computation | async-start | bytes 786432 | tf_op jit(solution)/shard_map/all_to_all | solution.py:199
  166.9 4.0 fusion.89
  170.8 4.6 fusion.37
  175.4 2.2 copy.244
  177.6 4.1 all-to-all-start.11
  181.8 3.0 convolution_convert_fusion.2
  184.8 2.2 copy.262
  187.0 4.6 fusion.40
  191.7 2.2 copy.253
  193.9 2.7 copy.283
  196.6 3.0 reshape.446
  199.6 2.7 copy.279
  202.4 3.0 reshape.443
  205.4 2.7 copy.280
  208.1 3.0 reshape.444
  211.1 2.7 copy.281
  213.9 3.0 reshape.445
  216.9 4.8 all-to-all-start.13
  221.7 4.5 fusion.90
  226.2 4.5 all-to-all-done.13
  230.7 4.1 all-to-all-start.15
  234.8 3.3 convolution_convert_fusion.4
  240.1 3.7 all-to-all-done.15
  243.8 5.9 all-to-all-start.14
  249.7 3.4 fusion.91
  253.1 6.6 %fusion.43 = bf16[2,6,64,256]{3,2,1,0:T(8,128)(2,1)} fusion(bf16[2,256,6,64]{1,3,2,0:T(8,128)(2,1)} %reshape.445, f32[2,6,256,256]{2,3,1,0:T(8,128)} %fusion.91, f32[2,6,256,256]{2,3,1,0:T(8,128)} %get-tuple-element.28, f32[2,6,256]{2,1,0:T(8,128)} %get-tuple-element.27), kind=kOutput, calls=%fused_computation.49 | convolution fusion | flops 106368256 | bytes 7090176 | tf_op jit(solution)/shard_map/bhqk,bkhd->bqhd/dot_general | solution.py:64
  261.6 5.7 all-to-all-start.9
  267.3 6.6 %fusion.46 = bf16[2,6,64,256]{3,2,1,0:T(8,128)(2,1)} fusion(bf16[2,256,6,64]{1,3,2,0:T(8,128)(2,1)} %reshape.444, f32[2,6,256,256]{2,3,1,0:T(8,128)} %fusion.91, f32[2,6,256,256]{2,3,1,0:T(8,128)} %get-tuple-element.28, f32[2,6,256]{2,1,0:T(8,128)} %get-tuple-element.27), kind=kOutput, calls=%fused_computation.50 | convolution fusion | flops 106368256 | bytes 7090176 | tf_op jit(solution)/shard_map/bhqk,bqhd->bkhd/dot_general | solution.py:70
  275.8 5.7 all-to-all-start.12
  295.8 2.2 fusion.22
  304.1 2.1 convolution_convert_fusion.3
  307.3 3.5 all-to-all-start.7
  310.8 2.3 convolution_convert_fusion.5
  314.2 6.9 %all-to-all-done.7 = bf16[1,64,1,8,384]{4,3,2,0,1:T(8,128)(2,1)S(1)} async-done(((bf16[1,64,1,8,384]{4,3,2,0,1:T(8,128)(2,1)}), bf16[1,64,1,8,384]{4,3,2,0,1:T(8,128)(2,1)S(1)}, u32[]{:S(2)}, u32[]{:S(2)}) %all-to-all-start.7) | async-done | bytes 393248 | tf_op jit(solution)/shard_map/all_to_all | solution.py:233
  321.1 5.1 all-to-all-start.3
  326.3 9.3 %all-to-all-done.3 = bf16[1,2,256,384]{3,1,0,2:T(2,128)(2,1)S(1)} async-done(((bf16[1,2,256,384]{3,1,0,2:T(2,128)(2,1)}), bf16[1,2,256,384]{3,1,0,2:T(2,128)(2,1)S(1)}, u32[]{:S(2)}, u32[]{:S(2)}) %all-to-all-start.3) | async-done | bytes 393248 | tf_op jit(solution)/shard_map/all_to_all | solution.py:211
  337.6 6.4 %reduce-scatter.4.cloned.1.call-done = bf16[1,64,768]{2,1,0:T(8,128)(2,1)} async-done(((bf16[1,512,768]{2,1,0:T(8,128)(2,1)}), bf16[1,64,768]{2,1,0:T(8,128)(2,1)}) %reduce-scatter.4.cloned.1.call-update) | async-done | bytes 98320 | tf_op jit(solution)/shard_map/reduce_scatter | solution.py:330
  352.4 5.5 bitcast_convert_fusion
  359.8 10.5 %all-reduce = bf16[768]{0:T(1024)(128)(2,1)S(1)} all-reduce(bf16[768]{0:T(1024)(128)(2,1)S(1)} %get-tuple-element.7), channel_id=5, replica_groups=mesh['dp'=4,'fy'=4,'fx'=8] {'dp'}, use_global_device_ids=true, to_apply=%region_19.20.clone | all-reduce | flops 768 | bytes 3072
  370.4 62.7 %psum.42 = bf16[192]{0:T(256)(128)(2,1)S(1)} all-reduce(bf16[192]{0:T(256)(128)(2,1)S(1)} %dynamic-slice.1), channel_id=1, replica_groups=mesh['dp'=4,'fy'=4,'fx'=8] {'fy','fx'}, use_global_device_ids=true, to_apply=%region_18.19 | all-reduce | flops 192 | bytes 768 | tf_op jit(solution)/shard_map/psum | solution.py:340
  433.7 2.9 fusion.23
  439.3 154.4 %psum.39 = f32[3,768]{1,0:T(4,128)S(1)} all-reduce(f32[3,768]{1,0:T(4,128)S(1)} %multiply_reduce_fusion.4), channel_id=1, replica_groups=mesh['dp'=4,'fy'=4,'fx'=8] {'dp','fx'}, use_global_device_ids=true, to_apply=%region_21.22 | all-reduce | flops 2304 | bytes 18432 | tf_op jit(solution)/shard_map/psum | solution.py:336
  596.3 2.5 convert_multiply_fusion
  (153 shorter events, 67.3 us)
Async XLA Ops:
  8.0 59.0 %copy-start = (bf16[768,2304]{1,0:T(8,128)(2,1)S(1)}, bf16[768,2304]{1,0:T(8,128)(2,1)}, u32[]{:S(2)}) copy-start(bf16[768,2304]{1,0:T(8,128)(2,1)} %param.15) | copy-start | bytes 10616836
  10.5 7.0 %copy-start.23 = (s32[1,16,8]{1,2,0:T(8,128)S(1)}, s32[1,16,8]{1,2,0:T(8,128)}, u32[]{:S(2)}) copy-start(s32[1,16,8]{1,2,0:T(8,128)} %param.10) | copy-start | bytes 1540
  10.5 7.5 %copy-start.27 = (s32[1,64]{1,0:T(1,128)S(1)}, s32[1,64]{1,0:T(1,128)}, u32[]{:S(2)}) copy-start(s32[1,64]{1,0:T(1,128)} %param.12) | copy-start | bytes 772
  12.2 58.9 %all-to-all-start.10 = ((bf16[1,16,4,8,384]{4,3,1,0,2:T(8,128)(2,1)}), bf16[1,16,4,8,384]{4,3,1,0,2:T(8,128)(2,1)}, u32[]{:S(2)}, u32[]{:S(2)}) async-start(bf16[1,16,4,8,384]{4,3,1,0,2:T(8,128)(2,1)} %copy.239), calls=%async_computation.10 | async-start | bytes 786432 | tf_op jit(solution)/shard_map/all_to_all | solution.py:273
  63.3 2.1 copy-start.2
  63.3 2.3 copy-start.12
  63.3 2.3 copy-start.25
  67.0 2.0 copy-start.21
  71.1 14.4 %all-to-all-start.6 = ((bf16[1,16,4,8,384]{4,3,1,0,2:T(8,128)(2,1)}), bf16[1,16,4,8,384]{4,3,1,0,2:T(8,128)(2,1)}, u32[]{:S(2)}, u32[]{:S(2)}) async-start(bf16[1,16,4,8,384]{4,3,1,0,2:T(8,128)(2,1)} %copy.224), calls=%async_computation.6 | async-start | bytes 786432 | tf_op jit(solution)/shard_map/all_to_all | solution.py:218
  85.5 13.1 %all-to-all-start.5 = ((bf16[1,16,4,8,384]{4,3,1,0,2:T(8,128)(2,1)}), bf16[1,16,4,8,384]{4,3,1,0,2:T(8,128)(2,1)}, u32[]{:S(2)}, u32[]{:S(2)}) async-start(bf16[1,16,4,8,384]{4,3,1,0,2:T(8,128)(2,1)} %copy.223), calls=%async_computation.5 | async-start | bytes 786432 | tf_op jit(solution)/shard_map/all_to_all | solution.py:215
  98.6 25.9 %copy-start.14 = (bf16[1,16,32,384]{3,2,1,0:T(8,128)(2,1)S(1)}, bf16[1,16,32,384]{3,2,1,0:T(8,128)(2,1)}, u32[]{:S(2)}) copy-start(bf16[1,16,32,384]{3,2,1,0:T(8,128)(2,1)} %get-tuple-element.15) | copy-start | bytes 1179652
  135.6 25.2 %all-to-all-start.1 = ((bf16[8,2,32,384]{3,2,1,0:T(8,128)(2,1)}), bf16[8,2,32,384]{3,2,1,0:T(8,128)(2,1)}, u32[]{:S(2)}, u32[]{:S(2)}) async-start(bf16[8,2,32,384]{3,2,1,0:T(8,128)(2,1)} %bitcast.250), calls=%async_computation.1 | async-start | bytes 786432 | tf_op jit(solution)/shard_map/all_to_all | solution.py:193
  160.7 16.9 %all-to-all-start = ((bf16[8,2,32,384]{3,2,1,0:T(8,128)(2,1)}), bf16[8,2,32,384]{3,2,1,0:T(8,128)(2,1)}, u32[]{:S(2)}, u32[]{:S(2)}) async-start(bf16[8,2,32,384]{3,2,1,0:T(8,128)(2,1)} %bitcast.249), calls=%async_computation | async-start | bytes 786432 | tf_op jit(solution)/shard_map/all_to_all | solution.py:199
  177.6 39.3 %all-to-all-start.11 = ((bf16[1,64,1,8,384]{4,3,2,0,1:T(8,128)(2,1)}), bf16[1,64,1,8,384]{4,3,2,0,1:T(8,128)(2,1)}, u32[]{:S(2)}, u32[]{:S(2)}) async-start(bf16[1,64,1,8,384]{4,3,2,0,1:T(8,128)(2,1)} %copy.244), calls=%async_computation.11 | async-start | bytes 786432 | tf_op jit(solution)/shard_map/all_to_all | solution.py:291
  216.9 13.8 %all-to-all-start.13 = ((bf16[1,64,1,8,384]{4,3,2,0,1:T(8,128)(2,1)}), bf16[1,64,1,8,384]{4,3,2,0,1:T(8,128)(2,1)}, u32[]{:S(2)}, u32[]{:S(2)}) async-start(bf16[1,64,1,8,384]{4,3,2,0,1:T(8,128)(2,1)} %copy.253), calls=%async_computation.13 | async-start | bytes 786432 | tf_op jit(solution)/shard_map/all_to_all | solution.py:292
  230.7 13.1 %all-to-all-start.15 = ((bf16[1,64,1,8,384]{4,3,2,0,1:T(8,128)(2,1)}), bf16[1,64,1,8,384]{4,3,2,0,1:T(8,128)(2,1)}, u32[]{:S(2)}, u32[]{:S(2)}) async-start(bf16[1,64,1,8,384]{4,3,2,0,1:T(8,128)(2,1)} %copy.262), calls=%async_computation.15 | async-start | bytes 786432 | tf_op jit(solution)/shard_map/all_to_all | solution.py:293
  243.8 17.8 %all-to-all-start.14 = ((bf16[1,2,256,384]{3,1,0,2:T(2,128)(2,1)}), bf16[1,2,256,384]{3,1,0,2:T(2,128)(2,1)}, u32[]{:S(2)}, u32[]{:S(2)}) async-start(bf16[1,2,256,384]{3,1,0,2:T(2,128)(2,1)} %copy.257), calls=%async_computation.14 | async-start | bytes 786432 | tf_op jit(solution)/shard_map/all_to_all | solution.py:262
  261.6 14.2 %all-to-all-start.9 = ((bf16[1,2,256,384]{3,1,0,2:T(2,128)(2,1)}), bf16[1,2,256,384]{3,1,0,2:T(2,128)(2,1)}, u32[]{:S(2)}, u32[]{:S(2)}) async-start(bf16[1,2,256,384]{3,1,0,2:T(2,128)(2,1)} %copy.236), calls=%async_computation.9 | async-start | bytes 786432 | tf_op jit(solution)/shard_map/all_to_all | solution.py:260
  275.8 16.9 %all-to-all-start.12 = ((bf16[1,2,256,384]{3,1,0,2:T(2,128)(2,1)}), bf16[1,2,256,384]{3,1,0,2:T(2,128)(2,1)}, u32[]{:S(2)}, u32[]{:S(2)}) async-start(bf16[1,2,256,384]{3,1,0,2:T(2,128)(2,1)} %copy.248), calls=%async_computation.12 | async-start | bytes 786432 | tf_op jit(solution)/shard_map/all_to_all | solution.py:261
  281.6 62.5 %reduce-scatter.4.cloned.1.call-start = ((), (), s32[]{:S(2)}) async-start(), calls=%async_computation.19 | async-start | bytes 884736 | tf_op jit(solution)/shard_map/reduce_scatter | solution.py:330
  292.7 1.2 copy-start.9
  292.7 1.3 copy-start.17
  293.8 1.1 copy-start.16
  293.9 1.1 copy-start.7
  293.9 1.2 copy-start.5
  294.0 1.2 copy-start.15
  294.1 1.7 copy-start.4
  294.1 1.7 copy-start.26
  295.8 2.2 copy-start.19
  302.6 1.5 copy-start.11
  302.6 1.5 copy-start.24
  306.2 4.6 copy-start.18
  306.2 4.6 copy-start.29
  307.3 13.8 %all-to-all-start.7 = ((bf16[1,64,1,8,384]{4,3,2,0,1:T(8,128)(2,1)}), bf16[1,64,1,8,384]{4,3,2,0,1:T(8,128)(2,1)S(1)}, u32[]{:S(2)}, u32[]{:S(2)}) async-start(bf16[1,64,1,8,384]{4,3,2,0,1:T(8,128)(2,1)} %copy.229), calls=%async_computation.7 | async-start | bytes 786432 | tf_op jit(solution)/shard_map/all_to_all | solution.py:233
  314.2 21.5 %copy-start.20 = (bf16[1,16,32,768]{3,2,1,0:T(8,128)(2,1)S(1)}, bf16[1,16,32,768]{3,2,1,0:T(8,128)(2,1)}, u32[]{:S(2)}) copy-start(bf16[1,16,32,768]{3,2,1,0:T(8,128)(2,1)} %param.17) | copy-start | bytes 2359300
  321.1 14.5 %all-to-all-start.3 = ((bf16[1,2,256,384]{3,1,0,2:T(2,128)(2,1)}), bf16[1,2,256,384]{3,1,0,2:T(2,128)(2,1)S(1)}, u32[]{:S(2)}, u32[]{:S(2)}) async-start(bf16[1,2,256,384]{3,1,0,2:T(2,128)(2,1)} %copy.219), calls=%async_computation.3 | async-start | bytes 786432 | tf_op jit(solution)/shard_map/all_to_all | solution.py:211
  326.2 110.4 %all-reduce.5.cloned.1.call-start = ((), (), s32[]{:S(2)}) async-start(), calls=%async_computation.20 | async-start | bytes 196608 | tf_op jit(solution)/shard_map/psum | solution.py:333
  335.8 8.3 %copy-start.10 = (bf16[8,1,2,32,384]{4,3,2,0,1:T(8,128)(2,1)S(1)}, bf16[8,1,2,32,384]{4,3,2,0,1:T(8,128)(2,1)}, u32[]{:S(2)}) copy-start(bf16[8,1,2,32,384]{4,3,2,0,1:T(8,128)(2,1)} %copy.238) | copy-start | bytes 1179652
  337.6 9.5 %copy-start.8 = (bf16[8,1,2,32,384]{4,3,2,0,1:T(8,128)(2,1)S(1)}, bf16[8,1,2,32,384]{4,3,2,0,1:T(8,128)(2,1)}, u32[]{:S(2)}) copy-start(bf16[8,1,2,32,384]{4,3,2,0,1:T(8,128)(2,1)} %copy-done.7) | copy-start | bytes 1179652
  344.0 94.2 %reduce-scatter.8.cloned.1.call-start = ((), (), s32[]{:S(2)}) async-start(), calls=%async_computation.22 | async-start | bytes 1474560 | tf_op jit(solution)/shard_map/reduce_scatter | solution.py:346
  345.0 4.8 copy-start.6
  345.0 93.2 %reduce-scatter.6.cloned.1.call-start = ((), (), s32[]{:S(2)}) async-start(), calls=%async_computation.21 | async-start | bytes 4423680 | tf_op jit(solution)/shard_map/reduce_scatter | solution.py:343
  347.1 5.3 copy-start.22
  357.9 0.7 copy-start.28
  357.9 75.8 %copy-start.3 = (f32[1,16,32,768]{3,2,1,0:T(8,128)S(1)}, f32[1,16,32,768]{3,2,1,0:T(8,128)}, u32[]{:S(2)}) copy-start(f32[1,16,32,768]{3,2,1,0:T(8,128)} %broadcast_in_dim.39) | copy-start | bytes 4718596
  357.9 75.8 %copy-start.13 = (bf16[1,16,32,768]{3,2,1,0:T(8,128)(2,1)S(1)}, bf16[1,16,32,768]{3,2,1,0:T(8,128)(2,1)}, u32[]{:S(2)}) copy-start(bf16[1,16,32,768]{3,2,1,0:T(8,128)(2,1)} %param.9) | copy-start | bytes 2359300
  357.9 236.4 %all-reduce.7.cloned.1.call-start = ((), (), s32[]{:S(2)}) async-start(), calls=%async_computation.23 | async-start | bytes 2359296 | tf_op jit(solution)/shard_map/psum | solution.py:338
  594.3 4.5 copy-start.1
Sparse Core Ops, SparseCore 0:
  303.7 40.2 reduce-scatter.3
  346.5 38.8 all-reduce.4
Sparse Core Ops, SparseCore 1:
  347.5 23.0 reduce-scatter.7
  372.9 41.1 reduce-scatter.5
  438.3 101.2 all-reduce.6
where the time goes:
time: 618 us; the launch traced here: 607 us
  blocking collectives  296 us (48%)
  local copies, waits for them, and re-layouts  97.6 us (16%)
  matrix products  65.2 us (11%)
  starting transfers between devices  64.2 us (10%)
  waiting for transfers between devices  45.4 us (7%)
  other arithmetic  20.7 us (3%)
  between operations  17 us (3%)
    psum x1, blocking collectives, local(): grad_level = lax.psum(level_part, ('dp', 'fx'))  154 us
    psum x1, blocking collectives, local(): lax.psum(grad_gain_local.astype(jnp.bfloat16), ('fy', 'fx'))  62.7 us
    all_gather x1, blocking collectives, local(): shard_piece = lax.all_gather(summary, 'fx', axis=1, tiled=True)  31.8 us
    reshape x8, local copies, waits for them, and re-layouts, rows_to_batch(): return tensor.reshape(tensor.shape[1], tensor.shape[2], -1, head_dim)  23 us
    another operation x7, local copies, waits for them, and re-layouts  17.7 us
    all_to_all x1, blocking collectives, local(): lax.all_to_all(to_column_groups(column_value, column_groups), 'fy', split...  13.2 us
    all_to_all x1, blocking collectives, local(): lax.all_to_all(to_row_groups(row_grad_out, row_groups), 'fx', split_axis=...  12.7 us
  transfers between devices with their start and end apart: 18, of which 7 were waited for; matrix products, arithmetic and copies ran while one was open for 27% of the time, Pallas kernels for 0%

commit v1 on v0

--- a/solution.py
+++ b/solution.py
@@ -333,7 +333,8 @@
         lambda part: part.astype(jnp.float32), lax.psum(as_sent(owned_rows), "fy")
     )
     level_part = jnp.sum(level_onehot[:, :, :, None] * grad_coarse[:, :, None, :], axis=(0, 1))
-    grad_level = lax.psum(level_part, ("dp", "fx"))
+    parts = lax.all_gather(level_part, ("dp", "fx"), axis=0, tiled=False)
+    grad_level = parts.sum(axis=0)
     summed = (
         lax.psum(grad_qkv_local.astype(jnp.bfloat16), ("fy", "fx")).astype(jnp.float32),
         lax.psum(grad_out_local.astype(jnp.bfloat16), ("fy", "fx")).astype(jnp.float32),

time: 618 us -> 596 us (0.964)
  blocking collectives: 296 us -> 225 us
  waiting for transfers between devices: 45.4 us -> 96 us
    psum x1 -> x0, blocking collectives: 154 us -> none  [local(): grad_level = lax.psum(level_part, ('dp', 'fx'))]
    all_gather x0 -> x1, blocking collectives: none -> 82.5 us  [local(): parts = lax.all_gather(level_part, ('dp', 'fx'), axis=0, tiled=False)]
    psum x1, waiting for transfers between devices: 0.01 us -> 34.6 us  [local(): lax.psum(as_sent(owned_rows), 'fy')]
    psum x1, waiting for transfers between devices: 0.01 us -> 22.4 us  [local(): lax.psum(grad_qkv_local.astype(jnp.bfloat16), ('fy', 'fx'))]
    reduce_scatter x1, waiting for transfers between devices: 6.4 us -> 0.01 us  [local(): lax.psum_scatter(as_sent(dense_sum), 'fx', scatter_dimension=1, tiled=True)]
  transfers between devices with their start and end apart: 18 -> 18, of which waited for: 7 -> 8; matrix products, arithmetic and copies ran while one was open for 27% -> 28% of each run, Pallas kernels for 0% -> 0%
where the time goes in v1:
time: 596 us; the launch traced here: 584 us
  blocking collectives  225 us (38%)
  local copies, waits for them, and re-layouts  97.7 us (16%)
  waiting for transfers between devices  96 us (16%)
  matrix products  65.2 us (11%)
  starting transfers between devices  64.2 us (11%)
  other arithmetic  20.8 us (3%)
  between operations  15.1 us (3%)
    all_gather x1, blocking collectives, local(): parts = lax.all_gather(level_part, ('dp', 'fx'), axis=0, tiled=False)  82.5 us
    psum x1, blocking collectives, local(): lax.psum(grad_gain_local.astype(jnp.bfloat16), ('fy', 'fx'))  63.6 us
    psum x1, waiting for transfers between devices, local(): lax.psum(as_sent(owned_rows), 'fy')  34.6 us
    all_gather x1, blocking collectives, local(): shard_piece = lax.all_gather(summary, 'fx', axis=1, tiled=True)  31.8 us
    reshape x8, local copies, waits for them, and re-layouts, rows_to_batch(): return tensor.reshape(tensor.shape[1], tensor.shape[2], -1, head_dim)  23 us
    psum x1, waiting for transfers between devices, local(): lax.psum(grad_qkv_local.astype(jnp.bfloat16), ('fy', 'fx'))  22.4 us
    another operation x7, local copies, waits for them, and re-layouts  17.7 us
    all_to_all x1, blocking collectives, local(): lax.all_to_all(to_column_groups(column_value, column_groups), 'fy', split...  13.2 us
  transfers between devices with their start and end apart: 18, of which 8 were waited for; matrix products, arithmetic and copies ran while one was open for 28% of the time, Pallas kernels for 0%

profile of v1, /device:TPU:0, one launch (start us, length us, event | category | flops | bytes accessed | tf_op | source)
XLA Modules:
  0.0 584.4 jit_solution(5938617024420577398)
XLA Ops:
  7.2 2.5 convolution_convert_fusion.1
  11.4 5.3 all-to-all-start.10
  22.5 31.8 %all_gather.9 = bf16[1,512,768]{2,1,0:T(8,128)(2,1)} all-gather(bf16[1,64,768]{2,1,0:T(8,128)(2,1)S(1)} %fusion.66), channel_id=1, replica_groups=mesh['dp'=4,'fy'=4,'fx'=8] {'fx'}, dimensions={1}, use_global_device_ids=true | all-gather | bytes 884736 | tf_op jit(solution)/shard_map/all_gather | solution.py:160
  54.3 2.8 gather_fusion
  59.7 2.8 broadcast_in_dim.39
  70.3 5.4 all-to-all-start.6
  77.5 7.2 %all-to-all-done.6 = bf16[1,16,4,8,384]{4,3,1,0,2:T(8,128)(2,1)} async-done(((bf16[1,16,4,8,384]{4,3,1,0,2:T(8,128)(2,1)}), bf16[1,16,4,8,384]{4,3,1,0,2:T(8,128)(2,1)}, u32[]{:S(2)}, u32[]{:S(2)}) %all-to-all-start.6) | async-done | bytes 393248 | tf_op jit(solution)/shard_map/all_to_all | solution.py:218
  84.7 4.1 all-to-all-start.5
  90.6 7.2 %all-to-all-done.5 = bf16[1,16,4,8,384]{4,3,1,0,2:T(8,128)(2,1)} async-done(((bf16[1,16,4,8,384]{4,3,1,0,2:T(8,128)(2,1)}), bf16[1,16,4,8,384]{4,3,1,0,2:T(8,128)(2,1)}, u32[]{:S(2)}, u32[]{:S(2)}) %all-to-all-start.5) | async-done | bytes 393248 | tf_op jit(solution)/shard_map/all_to_all | solution.py:215
  97.8 13.2 %all_to_all.270 = bf16[1,16,4,8,384]{4,3,1,0,2:T(8,128)(2,1)} all-to-all(bf16[1,16,4,8,384]{4,3,1,0,2:T(8,128)(2,1)} %copy.222), channel_id=1, replica_groups=mesh['dp'=4,'fy'=4,'fx'=8] {'fy'}, dimensions={2} | all-to-all | bytes 786432 | tf_op jit(solution)/shard_map/all_to_all | solution.py:221
  111.0 12.7 %all_to_all.271 = bf16[8,2,32,384]{3,2,1,0:T(8,128)(2,1)} all-to-all(bf16[8,2,32,384]{3,2,1,0:T(8,128)(2,1)} %bitcast.261), channel_id=1, replica_groups=mesh['dp'=4,'fy'=4,'fx'=8] {'fx'}, dimensions={0} | all-to-all | bytes 786432 | tf_op jit(solution)/shard_map/all_to_all | solution.py:246
  123.7 11.0 %all_to_all.272 = bf16[8,2,32,384]{3,2,1,0:T(8,128)(2,1)} all-to-all(bf16[8,2,32,384]{3,2,1,0:T(8,128)(2,1)S(1)} %bitcast.252), channel_id=1, replica_groups=mesh['dp'=4,'fy'=4,'fx'=8] {'fx'}, dimensions={0} | all-to-all | bytes 786432 | tf_op jit(solution)/shard_map/all_to_all | solution.py:196
  134.7 4.1 all-to-all-start.1
  138.8 2.4 reshape.396
  141.2 2.7 copy.260
  143.9 2.4 reshape.383
  146.3 2.5 reshape.385
  148.7 2.7 copy.251
  151.4 2.5 reshape.387
  153.9 2.7 copy.242
  156.6 3.3 fusion.59
  159.9 6.1 %all-to-all-start = ((bf16[8,2,32,384]{3,2,1,0:T(8,128)(2,1)}), bf16[8,2,32,384]{3,2,1,0:T(8,128)(2,1)}, u32[]{:S(2)}, u32[]{:S(2)}) async-start(bf16[8,2,32,384]{3,2,1,0:T(8,128)(2,1)} %bitcast.250), calls=%async_computation | async-start | bytes 786432 | tf_op jit(solution)/shard_map/all_to_all | solution.py:199
  166.0 4.0 fusion.89
  170.0 4.6 fusion.37
  174.6 2.2 copy.244
  176.8 4.1 all-to-all-start.11
  180.9 3.0 convolution_convert_fusion.2
  184.0 2.2 copy.262
  186.2 4.6 fusion.40
  190.8 2.2 copy.253
  193.1 2.7 copy.283
  195.8 3.0 reshape.450
  198.8 2.7 copy.279
  201.5 3.0 reshape.447
  204.6 2.7 copy.280
  207.3 3.0 reshape.448
  210.3 2.7 copy.281
  213.1 3.0 reshape.449
  216.1 4.8 all-to-all-start.13
  220.8 4.5 fusion.90
  225.4 4.5 all-to-all-done.13
  229.9 4.1 all-to-all-start.15
  234.0 3.3 convolution_convert_fusion.4
  239.2 3.7 all-to-all-done.15
  243.0 5.9 %all-to-all-start.14 = ((bf16[1,2,256,384]{3,1,0,2:T(2,128)(2,1)}), bf16[1,2,256,384]{3,1,0,2:T(2,128)(2,1)}, u32[]{:S(2)}, u32[]{:S(2)}) async-start(bf16[1,2,256,384]{3,1,0,2:T(2,128)(2,1)} %copy.257), calls=%async_computation.14 | async-start | bytes 786432 | tf_op jit(solution)/shard_map/all_to_all | solution.py:262
  248.9 3.4 fusion.91
  252.3 6.6 %fusion.43 = bf16[2,6,64,256]{3,2,1,0:T(8,128)(2,1)} fusion(bf16[2,256,6,64]{1,3,2,0:T(8,128)(2,1)} %reshape.449, f32[2,6,256,256]{2,3,1,0:T(8,128)} %fusion.91, f32[2,6,256,256]{2,3,1,0:T(8,128)} %get-tuple-element.28, f32[2,6,256]{2,1,0:T(8,128)} %get-tuple-element.27), kind=kOutput, calls=%fused_computation.49 | convolution fusion | flops 106368256 | bytes 7090176 | tf_op jit(solution)/shard_map/bhqk,bkhd->bqhd/dot_general | solution.py:64
  260.8 5.7 all-to-all-start.9
  266.5 6.6 %fusion.46 = bf16[2,6,64,256]{3,2,1,0:T(8,128)(2,1)} fusion(bf16[2,256,6,64]{1,3,2,0:T(8,128)(2,1)} %reshape.448, f32[2,6,256,256]{2,3,1,0:T(8,128)} %fusion.91, f32[2,6,256,256]{2,3,1,0:T(8,128)} %get-tuple-element.28, f32[2,6,256]{2,1,0:T(8,128)} %get-tuple-element.27), kind=kOutput, calls=%fused_computation.50 | convolution fusion | flops 106368256 | bytes 7090176 | tf_op jit(solution)/shard_map/bhqk,bqhd->bkhd/dot_general | solution.py:70
  275.1 5.7 all-to-all-start.12
  295.0 2.2 fusion.22
  306.5 3.5 all-to-all-start.7
  310.0 2.3 convolution_convert_fusion.5
  313.4 6.9 %all-to-all-done.7 = bf16[1,64,1,8,384]{4,3,2,0,1:T(8,128)(2,1)S(1)} async-done(((bf16[1,64,1,8,384]{4,3,2,0,1:T(8,128)(2,1)}), bf16[1,64,1,8,384]{4,3,2,0,1:T(8,128)(2,1)S(1)}, u32[]{:S(2)}, u32[]{:S(2)}) %all-to-all-start.7) | async-done | bytes 393248 | tf_op jit(solution)/shard_map/all_to_all | solution.py:233
  320.3 5.1 all-to-all-start.3
  325.5 9.3 %all-to-all-done.3 = bf16[1,2,256,384]{3,1,0,2:T(2,128)(2,1)S(1)} async-done(((bf16[1,2,256,384]{3,1,0,2:T(2,128)(2,1)}), bf16[1,2,256,384]{3,1,0,2:T(2,128)(2,1)S(1)}, u32[]{:S(2)}, u32[]{:S(2)}) %all-to-all-start.3) | async-done | bytes 393248 | tf_op jit(solution)/shard_map/all_to_all | solution.py:211
  345.2 5.5 bitcast_convert_fusion
  352.5 10.5 %all-reduce = bf16[768]{0:T(1024)(128)(2,1)S(1)} all-reduce(bf16[768]{0:T(1024)(128)(2,1)S(1)} %get-tuple-element.7), channel_id=6, replica_groups=mesh['dp'=4,'fy'=4,'fx'=8] {'dp'}, use_global_device_ids=true, to_apply=%region_19.20.clone | all-reduce | flops 768 | bytes 3072
  363.1 63.6 %psum.34 = bf16[192]{0:T(256)(128)(2,1)S(1)} all-reduce(bf16[192]{0:T(256)(128)(2,1)S(1)} %dynamic-slice.1), channel_id=1, replica_groups=mesh['dp'=4,'fy'=4,'fx'=8] {'fy','fx'}, use_global_device_ids=true, to_apply=%region_18.19 | all-reduce | flops 192 | bytes 768 | tf_op jit(solution)/shard_map/psum | solution.py:341
  426.7 2.9 fusion.23
  430.3 34.6 %all-reduce.5.cloned.1.call-done = bf16[1,64,768]{2,1,0:T(8,128)(2,1)} async-done(((bf16[1,64,768]{2,1,0:T(8,128)(2,1)}), bf16[1,64,768]{2,1,0:T(8,128)(2,1)}) %all-reduce.5.cloned.1.call-update) | async-done | bytes 98320 | tf_op jit(solution)/shard_map/psum | solution.py:333
  466.0 82.5 %all-gather.1 = f32[32,3,768]{2,1,0:T(4,128)S(1)} all-gather(f32[1,3,768]{2,1,0:T(4,128)S(1)} %bitcast.281), channel_id=2, replica_groups=mesh['dp'=4,'fy'=4,'fx'=8] {'dp','fx'}, dimensions={0}, use_global_device_ids=true | all-gather | bytes 304128 | tf_op jit(solution)/shard_map/all_gather | solution.py:336
  550.8 22.4 %all-reduce.7.cloned.1.call-done = (bf16[192,2304]{1,0:T(8,128)(2,1)}, bf16[192,768]{1,0:T(8,128)(2,1)}) async-done(((bf16[192,2304]{1,0:T(8,128)(2,1)}, bf16[192,768]{1,0:T(8,128)(2,1)}), (bf16[192,2304]{1,0:T(8,128)(2,1)}, bf16[192,768]{1,0:T(8,128)(2,1)})) %all-reduce.7.cloned.1.call-update) | async-done | bytes 1179664 | tf_op jit(solution)/shard_map/psum | solution.py:339
  575.1 2.5 convert_multiply_fusion
  (154 shorter events, 69.5 us)
Async XLA Ops:
  7.2 59.0 %copy-start = (bf16[768,2304]{1,0:T(8,128)(2,1)S(1)}, bf16[768,2304]{1,0:T(8,128)(2,1)}, u32[]{:S(2)}) copy-start(bf16[768,2304]{1,0:T(8,128)(2,1)} %param.15) | copy-start | bytes 10616836
  9.7 7.0 %copy-start.23 = (s32[1,16,8]{1,2,0:T(8,128)S(1)}, s32[1,16,8]{1,2,0:T(8,128)}, u32[]{:S(2)}) copy-start(s32[1,16,8]{1,2,0:T(8,128)} %param.10) | copy-start | bytes 1540
  9.7 7.5 %copy-start.27 = (s32[1,64]{1,0:T(1,128)S(1)}, s32[1,64]{1,0:T(1,128)}, u32[]{:S(2)}) copy-start(s32[1,64]{1,0:T(1,128)} %param.12) | copy-start | bytes 772
  11.4 58.9 %all-to-all-start.10 = ((bf16[1,16,4,8,384]{4,3,1,0,2:T(8,128)(2,1)}), bf16[1,16,4,8,384]{4,3,1,0,2:T(8,128)(2,1)}, u32[]{:S(2)}, u32[]{:S(2)}) async-start(bf16[1,16,4,8,384]{4,3,1,0,2:T(8,128)(2,1)} %copy.239), calls=%async_computation.10 | async-start | bytes 786432 | tf_op jit(solution)/shard_map/all_to_all | solution.py:273
  62.4 2.1 copy-start.2
  62.5 2.3 copy-start.12
  62.5 2.3 copy-start.25
  66.2 2.0 copy-start.21
  70.3 14.4 %all-to-all-start.6 = ((bf16[1,16,4,8,384]{4,3,1,0,2:T(8,128)(2,1)}), bf16[1,16,4,8,384]{4,3,1,0,2:T(8,128)(2,1)}, u32[]{:S(2)}, u32[]{:S(2)}) async-start(bf16[1,16,4,8,384]{4,3,1,0,2:T(8,128)(2,1)} %copy.224), calls=%async_computation.6 | async-start | bytes 786432 | tf_op jit(solution)/shard_map/all_to_all | solution.py:218
  84.7 13.1 %all-to-all-start.5 = ((bf16[1,16,4,8,384]{4,3,1,0,2:T(8,128)(2,1)}), bf16[1,16,4,8,384]{4,3,1,0,2:T(8,128)(2,1)}, u32[]{:S(2)}, u32[]{:S(2)}) async-start(bf16[1,16,4,8,384]{4,3,1,0,2:T(8,128)(2,1)} %copy.223), calls=%async_computation.5 | async-start | bytes 786432 | tf_op jit(solution)/shard_map/all_to_all | solution.py:215
  97.8 25.9 %copy-start.14 = (bf16[1,16,32,384]{3,2,1,0:T(8,128)(2,1)S(1)}, bf16[1,16,32,384]{3,2,1,0:T(8,128)(2,1)}, u32[]{:S(2)}) copy-start(bf16[1,16,32,384]{3,2,1,0:T(8,128)(2,1)} %get-tuple-element.15) | copy-start | bytes 1179652
  134.7 25.2 %all-to-all-start.1 = ((bf16[8,2,32,384]{3,2,1,0:T(8,128)(2,1)}), bf16[8,2,32,384]{3,2,1,0:T(8,128)(2,1)}, u32[]{:S(2)}, u32[]{:S(2)}) async-start(bf16[8,2,32,384]{3,2,1,0:T(8,128)(2,1)} %bitcast.251), calls=%async_computation.1 | async-start | bytes 786432 | tf_op jit(solution)/shard_map/all_to_all | solution.py:193
  159.9 16.9 %all-to-all-start = ((bf16[8,2,32,384]{3,2,1,0:T(8,128)(2,1)}), bf16[8,2,32,384]{3,2,1,0:T(8,128)(2,1)}, u32[]{:S(2)}, u32[]{:S(2)}) async-start(bf16[8,2,32,384]{3,2,1,0:T(8,128)(2,1)} %bitcast.250), calls=%async_computation | async-start | bytes 786432 | tf_op jit(solution)/shard_map/all_to_all | solution.py:199
  176.8 39.3 %all-to-all-start.11 = ((bf16[1,64,1,8,384]{4,3,2,0,1:T(8,128)(2,1)}), bf16[1,64,1,8,384]{4,3,2,0,1:T(8,128)(2,1)}, u32[]{:S(2)}, u32[]{:S(2)}) async-start(bf16[1,64,1,8,384]{4,3,2,0,1:T(8,128)(2,1)} %copy.244), calls=%async_computation.11 | async-start | bytes 786432 | tf_op jit(solution)/shard_map/all_to_all | solution.py:291
  216.1 13.8 %all-to-all-start.13 = ((bf16[1,64,1,8,384]{4,3,2,0,1:T(8,128)(2,1)}), bf16[1,64,1,8,384]{4,3,2,0,1:T(8,128)(2,1)}, u32[]{:S(2)}, u32[]{:S(2)}) async-start(bf16[1,64,1,8,384]{4,3,2,0,1:T(8,128)(2,1)} %copy.253), calls=%async_computation.13 | async-start | bytes 786432 | tf_op jit(solution)/shard_map/all_to_all | solution.py:292
  229.9 13.1 %all-to-all-start.15 = ((bf16[1,64,1,8,384]{4,3,2,0,1:T(8,128)(2,1)}), bf16[1,64,1,8,384]{4,3,2,0,1:T(8,128)(2,1)}, u32[]{:S(2)}, u32[]{:S(2)}) async-start(bf16[1,64,1,8,384]{4,3,2,0,1:T(8,128)(2,1)} %copy.262), calls=%async_computation.15 | async-start | bytes 786432 | tf_op jit(solution)/shard_map/all_to_all | solution.py:293
  243.0 17.9 %all-to-all-start.14 = ((bf16[1,2,256,384]{3,1,0,2:T(2,128)(2,1)}), bf16[1,2,256,384]{3,1,0,2:T(2,128)(2,1)}, u32[]{:S(2)}, u32[]{:S(2)}) async-start(bf16[1,2,256,384]{3,1,0,2:T(2,128)(2,1)} %copy.257), calls=%async_computation.14 | async-start | bytes 786432 | tf_op jit(solution)/shard_map/all_to_all | solution.py:262
  260.8 14.2 %all-to-all-start.9 = ((bf16[1,2,256,384]{3,1,0,2:T(2,128)(2,1)}), bf16[1,2,256,384]{3,1,0,2:T(2,128)(2,1)}, u32[]{:S(2)}, u32[]{:S(2)}) async-start(bf16[1,2,256,384]{3,1,0,2:T(2,128)(2,1)} %copy.236), calls=%async_computation.9 | async-start | bytes 786432 | tf_op jit(solution)/shard_map/all_to_all | solution.py:260
  275.1 16.9 %all-to-all-start.12 = ((bf16[1,2,256,384]{3,1,0,2:T(2,128)(2,1)}), bf16[1,2,256,384]{3,1,0,2:T(2,128)(2,1)}, u32[]{:S(2)}, u32[]{:S(2)}) async-start(bf16[1,2,256,384]{3,1,0,2:T(2,128)(2,1)} %copy.248), calls=%async_computation.12 | async-start | bytes 786432 | tf_op jit(solution)/shard_map/all_to_all | solution.py:261
  280.8 148.9 %reduce-scatter.4.cloned.1.call-start = ((), (), s32[]{:S(2)}) async-start(), calls=%async_computation.19 | async-start | bytes 884736 | tf_op jit(solution)/shard_map/reduce_scatter | solution.py:330
  291.9 1.2 copy-start.9
  291.9 1.3 copy-start.17
  293.0 1.1 copy-start.16
  293.1 1.1 copy-start.7
  293.1 1.2 copy-start.5
  293.2 1.2 copy-start.15
  293.3 1.7 copy-start.4
  293.3 1.7 copy-start.26
  295.0 2.2 copy-start.19
  301.8 1.5 copy-start.11
  301.8 1.5 copy-start.24
  305.4 4.6 copy-start.18
  305.4 4.6 copy-start.29
  306.5 13.8 %all-to-all-start.7 = ((bf16[1,64,1,8,384]{4,3,2,0,1:T(8,128)(2,1)}), bf16[1,64,1,8,384]{4,3,2,0,1:T(8,128)(2,1)S(1)}, u32[]{:S(2)}, u32[]{:S(2)}) async-start(bf16[1,64,1,8,384]{4,3,2,0,1:T(8,128)(2,1)} %copy.229), calls=%async_computation.7 | async-start | bytes 786432 | tf_op jit(solution)/shard_map/all_to_all | solution.py:233
  313.4 21.5 %copy-start.10 = (bf16[8,1,2,32,384]{4,3,2,0,1:T(8,128)(2,1)S(1)}, bf16[8,1,2,32,384]{4,3,2,0,1:T(8,128)(2,1)}, u32[]{:S(2)}) copy-start(bf16[8,1,2,32,384]{4,3,2,0,1:T(8,128)(2,1)} %copy.238) | copy-start | bytes 1179652
  320.3 14.5 %all-to-all-start.3 = ((bf16[1,2,256,384]{3,1,0,2:T(2,128)(2,1)}), bf16[1,2,256,384]{3,1,0,2:T(2,128)(2,1)S(1)}, u32[]{:S(2)}, u32[]{:S(2)}) async-start(bf16[1,2,256,384]{3,1,0,2:T(2,128)(2,1)} %copy.219), calls=%async_computation.3 | async-start | bytes 786432 | tf_op jit(solution)/shard_map/all_to_all | solution.py:211
  325.4 104.9 %reduce-scatter.8.cloned.1.call-start = ((), (), s32[]{:S(2)}) async-start(), calls=%async_computation.22 | async-start | bytes 1474560 | tf_op jit(solution)/shard_map/reduce_scatter | solution.py:347
  325.5 10.4 %copy-start.20 = (bf16[1,16,32,768]{3,2,1,0:T(8,128)(2,1)S(1)}, bf16[1,16,32,768]{3,2,1,0:T(8,128)(2,1)}, u32[]{:S(2)}) copy-start(bf16[1,16,32,768]{3,2,1,0:T(8,128)(2,1)} %param.17) | copy-start | bytes 2359300
  337.7 2.1 copy-start.8
  337.7 4.8 copy-start.6
  337.7 92.6 %reduce-scatter.6.cloned.1.call-start = ((), (), s32[]{:S(2)}) async-start(), calls=%async_computation.21 | async-start | bytes 4423680 | tf_op jit(solution)/shard_map/reduce_scatter | solution.py:344
  339.8 5.3 copy-start.22
  350.6 0.7 copy-start.28
  350.6 76.1 %copy-start.3 = (f32[1,16,32,768]{3,2,1,0:T(8,128)S(1)}, f32[1,16,32,768]{3,2,1,0:T(8,128)}, u32[]{:S(2)}) copy-start(f32[1,16,32,768]{3,2,1,0:T(8,128)} %broadcast_in_dim.39) | copy-start | bytes 4718596
  350.6 76.1 %copy-start.13 = (bf16[1,16,32,768]{3,2,1,0:T(8,128)(2,1)S(1)}, bf16[1,16,32,768]{3,2,1,0:T(8,128)(2,1)}, u32[]{:S(2)}) copy-start(bf16[1,16,32,768]{3,2,1,0:T(8,128)(2,1)} %param.9) | copy-start | bytes 2359300
  350.6 114.3 %all-reduce.5.cloned.1.call-start = ((), (), s32[]{:S(2)}) async-start(), calls=%async_computation.20 | async-start | bytes 196608 | tf_op jit(solution)/shard_map/psum | solution.py:333
  429.7 143.5 %all-reduce.7.cloned.1.call-start = ((), (), s32[]{:S(2)}) async-start(), calls=%async_computation.23 | async-start | bytes 2359296 | tf_op jit(solution)/shard_map/psum | solution.py:339
  573.2 4.5 copy-start.1
Sparse Core Ops, SparseCore 0:
  302.9 40.2 reduce-scatter.3
  346.2 23.0 reduce-scatter.7
  371.8 41.1 reduce-scatter.5
  429.8 35.0 all-reduce.4
  468.1 104.9 all-reduce.6
